TPU v7x, 512 devices: a whole 4x4x16 slice. The times are simulated.
512 devices in a mesh: dp: 16 (over y, x), expert: 32 (over z, core).
Axes of the slice: x: 4, y: 4, z: 16, core: 2. Of those that a mesh axis runs over, the one named last changes fastest.
Arguments:
- cotangent: bfloat16 [65536, 4096], P(('dp', 'expert')), may hold values from -0.59765625 to 0.59765625
- expert_ids: int32 [65536, 8], P(('dp', 'expert')), may hold values from 0 to 63, all different within a row; in each aligned block of 128 rows (0 to 127, 128 to 255, ...) at most 20 rows name the same one
- gates: bfloat16 [65536, 8], P(('dp', 'expert')), may hold values from 0.019897461 to 0.5
- hidden: bfloat16 [64, 16, 640, 1536], P('expert', 'dp'), may hold values from -6 to 6
- q_prev: bfloat16 [64, 4096, 64], P('expert', 'dp'), may hold values from -0.09375 to 0.09375
Outputs:
- p_merged: float32 [64, 1536, 64], P('expert', 'dp')
- q_next: float32 [64, 4096, 64], P('expert', 'dp')
Inputs may be any that keep to these rules, and one draw needn't show every extreme that they name: `expert_ids`: each row names 8 different experts. Within the 128 rows of one device no expert is named by more than 20 rows, a bound that some block reaches.
All inputs are finite; a program needn't handle non-finite values.
Results may differ from a plain program's by a relative error of at most 0.0056.
Values may be sent and summed in bfloat16 or wider, within the bound.
A program may use at most 128 MiB of HBM per device.

v0:
```python
import jax
import jax.numpy as jnp
from jax import lax
from jax.sharding import PartitionSpec as P


def slot_positions(expert_ids, experts_all):
    flat_ids = expert_ids.reshape(-1)
    labels = jnp.arange(experts_all, dtype=jnp.int32)
    onehot = (labels[:, None] == flat_ids[None, :]).astype(jnp.bfloat16)
    positions = jnp.arange(flat_ids.shape[0], dtype=jnp.int32)
    upper_mask = (positions[:, None] < positions[None, :]).astype(jnp.bfloat16)
    earlier = jnp.dot(onehot, upper_mask, preferred_element_type=jnp.float32)
    slot_index = jnp.sum(earlier * onehot.astype(jnp.float32), axis=0)
    return slot_index.astype(jnp.int32).reshape(expert_ids.shape)


def selection(target, gate_values, row_total):
    row_labels = jnp.arange(row_total, dtype=jnp.int32)[:, None]
    chooser = jnp.zeros((row_total, target.shape[0]), jnp.bfloat16)
    for column in range(target.shape[1]):
        hit = row_labels == target[:, column][None, :]
        chooser = chooser + jnp.where(
            hit, gate_values[:, column][None, :], jnp.zeros((), jnp.bfloat16)
        )
    return chooser


def whiten(gram_matrix, factor):
    lower_factor = jnp.linalg.cholesky(gram_matrix)

    def solve_one(lower_one, block_rhs):
        return jax.scipy.linalg.solve_triangular(lower_one, block_rhs, lower=True)

    solved = jax.vmap(solve_one)(lower_factor, jnp.swapaxes(factor, 1, 2))
    return jnp.swapaxes(solved, 1, 2).astype(jnp.bfloat16)


def local(cotangent, expert_ids, gates, hidden, q_prev):
    groups = lax.axis_size("expert")
    held_experts = hidden.shape[0]
    capacity = hidden.shape[2] // groups
    experts_all = held_experts * groups
    slot_count = groups * capacity
    model_width = cotangent.shape[1]
    row_total = held_experts * slot_count
    slot_index = slot_positions(expert_ids, experts_all)
    target = (
        expert_ids % held_experts * slot_count + expert_ids // held_experts * capacity + slot_index
    )
    chooser = selection(target, gates, row_total)
    outgoing = jnp.dot(chooser, cotangent, preferred_element_type=jnp.float32).astype(jnp.bfloat16)
    outgoing = outgoing.reshape(held_experts, groups, capacity, model_width)
    arrived = lax.all_to_all(outgoing, "expert", split_axis=1, concat_axis=1, tiled=True)
    dispatched = arrived.reshape(held_experts, slot_count, model_width)
    whole_factor = lax.all_gather(q_prev, "dp", axis=1, tiled=True)
    projected = jnp.einsum(
        "esd,edr->esr", dispatched, whole_factor, preferred_element_type=jnp.float32
    ).astype(jnp.bfloat16)
    own_hidden = hidden[:, 0]
    partial_value = jnp.einsum(
        "esf,esr->efr", own_hidden, projected, preferred_element_type=jnp.float32
    )
    members = lax.axis_size("dp")
    dp_index = lax.axis_index("dp")
    hidden_width = own_hidden.shape[2]
    share_rows = hidden_width // members
    merged = lax.psum(partial_value, "dp")
    gram_matrix = jnp.einsum("efr,efs->ers", merged, merged, precision=lax.Precision.HIGHEST)
    basis_rows = whiten(gram_matrix, merged)
    p_share = lax.dynamic_slice_in_dim(merged, dp_index * share_rows, share_rows, 1)
    mapped = jnp.einsum(
        "esf,efr->esr", own_hidden, basis_rows, preferred_element_type=jnp.float32
    ).astype(jnp.bfloat16)
    width_rows = model_width // members
    q_part = jnp.einsum("esd,esr->edr", dispatched, mapped, preferred_element_type=jnp.float32)
    q_summed = lax.psum(q_part, "dp")
    q_share = lax.dynamic_slice_in_dim(q_summed, dp_index * width_rows, width_rows, 1)
    return (p_share, q_share)


def solution(mesh):
    placed = (
        P(("dp", "expert"), None),
        P(("dp", "expert"), None),
        P(("dp", "expert"), None),
        P("expert", "dp", None, None),
        P("expert", "dp", None),
    )
    return jax.shard_map(
        local,
        mesh=mesh,
        in_specs=placed,
        out_specs=(P("expert", "dp", None), P("expert", "dp", None)),
        check_vma=False,
    )
```

profile of v0, /device:TPU:6, one launch (start us, length us, event | category | flops | bytes accessed | tf_op | source)
XLA Modules:
  0.0 827.8 jit_solution(4935514527823052235)
XLA Ops:
  7.2 0.0 copy-start
  7.2 0.9 copy.36
  8.1 0.1 eq.139
  8.1 0.4 fusion.19
  8.6 0.1 convert_element_type.30
  8.7 0.1 fusion.68
  8.7 0.4 slice_reduce_fusion.7
  9.1 1.0 slice_bitcast_fusion.7
  10.1 0.0 copy-done
  10.1 5.7 convolution_convert_fusion
  15.7 13.9 %reshape.41 = bf16[2,32,20,4096]{3,2,1,0:T(8,128)(2,1)} reshape(bf16[1280,4096]{1,0:T(8,128)(2,1)} %convolution_convert_fusion) | data formatting | bytes 20971520 | tf_op jit(solution)/shard_map/reshape | solution.py:53
  29.7 19.5 %copy.41 = bf16[2,32,20,4096]{3,0,2,1:T(2,128)(2,1)} copy(bf16[2,32,20,4096]{3,2,1,0:T(8,128)(2,1)} %reshape.41) | data formatting | bytes 20971520 | tf_op jit(solution)/shard_map/reshape | solution.py:53
  49.2 15.6 %all-to-all-start = ((bf16[2,32,20,4096]{3,0,2,1:T(2,128)(2,1)}), bf16[2,32,20,4096]{3,0,2,1:T(2,128)(2,1)}, u32[]{:S(2)}, u32[]{:S(2)}) async-start(bf16[2,32,20,4096]{3,0,2,1:T(2,128)(2,1)} %copy.41), calls=%async_computation | async-start | bytes 20971520 | tf_op jit(solution)/shard_map/all_to_all | solution.py:54
  64.8 0.0 all-gather.2.cloned.1.call-start
  64.9 0.7 all-gather.2.cloned.1.call-update
  65.6 0.2 all-reduce.3.cloned.1.call-start
  65.8 62.0 %all-gather.2.cloned.1.call-done = bf16[2,4096,64]{1,2,0:T(8,128)(2,1)} async-done(((bf16[2,256,64]{1,2,0:T(8,128)(2,1)}), bf16[2,4096,64]{1,2,0:T(8,128)(2,1)}) %all-gather.2.cloned.1.call-update) | async-done | bytes 1048592 | tf_op jit(solution)/shard_map/all_gather | solution.py:56
  127.8 389.7 %all-to-all-done = bf16[2,32,20,4096]{3,0,2,1:T(2,128)(2,1)} async-done(((bf16[2,32,20,4096]{3,0,2,1:T(2,128)(2,1)}), bf16[2,32,20,4096]{3,0,2,1:T(2,128)(2,1)}, u32[]{:S(2)}, u32[]{:S(2)}) %all-to-all-start) | async-done | bytes 10485792 | tf_op jit(solution)/shard_map/all_to_all | solution.py:54
  517.5 18.4 %fusion.9 = f32[2,1536,64]{1,2,0:T(8,128)} fusion(bf16[2,1,640,1536]{3,2,1,0:T(8,128)(2,1)} %param.8, bf16[2,4096,64]{1,2,0:T(8,128)(2,1)} %all-gather.2.cloned.1.call-done, bf16[2,640,4096]{2,0,1:T(2,128)(2,1)} %bitcast.8), kind=kOutput, calls=%fused_computation.11 | convolution fusion | flops 922828800 | bytes 16252928 | tf_op jit(solution)/shard_map/esf,esr->efr/dot_general | solution.py:61
  535.9 0.0 all-reduce.3.cloned.1.call-update
  536.0 0.0 all-reduce.5.cloned.1.call-start
  536.0 116.5 %all-reduce.3.cloned.1.call-done = f32[2,1536,64]{1,2,0:T(8,128)} async-done(((f32[2,1536,64]{1,2,0:T(8,128)}), f32[2,1536,64]{1,2,0:T(8,128)}) %all-reduce.3.cloned.1.call-update) | async-done | bytes 786448 | tf_op jit(solution)/shard_map/psum | solution.py:68
  652.6 2.2 fusion.77
  654.8 0.1 copy.43
  654.9 11.7 %custom-call.8 = f32[2,64,64]{2,1,0:T(8,128)S(1)} custom-call(f32[2,64,64]{2,1,0:T(8,128)S(1)} %fusion.71), custom_call_target="Cholesky" | custom-call | tf_op jit(solution)/shard_map/jit(cholesky)/cholesky | solution.py:30
  666.7 0.1 compare_reduce_fusion
  666.8 0.1 select_bitcast_fusion
  666.9 10.0 %custom-call.9 = f32[2,1,64,64]{2,3,1,0:T(8,128)S(1)} custom-call(f32[2,1,64,64]{3,2,1,0:T(8,128)S(1)} %select_bitcast_fusion), custom_call_target="InvertDiagBlocksLowerTriangular" | custom-call | tf_op jit(solution)/shard_map/vmap(jit(_solve_triangular))/triangular_solve | solution.py:33
  676.9 2.0 convolution_convert_fusion.1
  678.9 19.2 %fusion = f32[2,4096,64]{1,2,0:T(8,128)} fusion(bf16[2,640,4096]{2,0,1:T(2,128)(2,1)} %bitcast.8, bf16[2,1536,64]{1,2,0:T(8,128)(2,1)S(1)} %convolution_convert_fusion.1, bf16[2,1,640,1536]{3,2,1,0:T(8,128)(2,1)} %param.8), kind=kOutput, calls=%fused_computation.1 | convolution fusion | flops 922828800 | bytes 16908288 | tf_op jit(solution)/shard_map/esd,esr->edr/dot_general | solution.py:76
  698.1 0.0 all-reduce.5.cloned.1.call-update
  698.1 1.6 constant_dynamic-slice_fusion.1
  699.8 120.0 %all-reduce.5.cloned.1.call-done = f32[2,4096,64]{1,2,0:T(8,128)} async-done(((f32[2,4096,64]{1,2,0:T(8,128)}), f32[2,4096,64]{1,2,0:T(8,128)}) %all-reduce.5.cloned.1.call-update) | async-done | bytes 2097168 | tf_op jit(solution)/shard_map/psum | solution.py:77
  819.7 1.6 constant_dynamic-slice_fusion
  (5 shorter events, 0.1 us)
Async XLA Ops:
  7.2 2.9 copy-start
  49.2 468.3 %all-to-all-start = ((bf16[2,32,20,4096]{3,0,2,1:T(2,128)(2,1)}), bf16[2,32,20,4096]{3,0,2,1:T(2,128)(2,1)}, u32[]{:S(2)}, u32[]{:S(2)}) async-start(bf16[2,32,20,4096]{3,0,2,1:T(2,128)(2,1)} %copy.41), calls=%async_computation | async-start | bytes 20971520 | tf_op jit(solution)/shard_map/all_to_all | solution.py:54
  64.8 63.0 %all-gather.2.cloned.1.call-start = ((), (), s32[]{:S(2)}) async-start(), calls=%async_computation.1 | async-start | bytes 1114112 | tf_op jit(solution)/shard_map/all_gather | solution.py:56
  65.6 587.0 %all-reduce.3.cloned.1.call-start = ((), (), s32[]{:S(2)}) async-start(), calls=%async_computation.2 | async-start | bytes 1572864 | tf_op jit(solution)/shard_map/psum | solution.py:68
  536.0 283.7 %all-reduce.5.cloned.1.call-start = ((), (), s32[]{:S(2)}) async-start(), calls=%async_computation.3 | async-start | bytes 4194304 | tf_op jit(solution)/shard_map/psum | solution.py:77
Sparse Core Ops, SparseCore 0:
  68.6 59.1 all-gather.1
  536.1 116.4 all-reduce.2
  698.2 121.4 all-reduce.4
where the time goes:
time: 829 us; the launch traced here: 828 us
  waiting for transfers between devices  689 us (83%)
  matrix products  47.8 us (6%)
  local copies, waits for them, and re-layouts  39.2 us (5%)
  other arithmetic  22.1 us (3%)
  starting transfers between devices  15.9 us (2%)
  between operations  13.9 us (2%)
    all_to_all x1, waiting for transfers between devices, local(): lax.all_to_all(outgoing, 'expert', split_axis=1, concat_axis=1, tiled=True)  390 us
    psum x1, waiting for transfers between devices, local(): q_summed = lax.psum(q_part, 'dp')  120 us
    psum x1, waiting for transfers between devices, local(): merged = lax.psum(partial_value, 'dp')  117 us
    all_gather x1, waiting for transfers between devices, local(): whole_factor = lax.all_gather(q_prev, 'dp', axis=1, tiled=True)  62 us
    reshape x2, local copies, waits for them, and re-layouts, local(): outgoing = outgoing.reshape(held_experts, groups, capacity, model_width)  33.5 us
    dot_general x1, matrix products, local(): jnp.einsum('esd,esr->edr', dispatched, mapped, preferred_element_type=jnp...  19.2 us
    dot_general x1, matrix products, local(): jnp.einsum('esf,esr->efr', own_hidden, projected, preferred_element_type=...  18.4 us
  transfers between devices with their start and end apart: 4, of which 4 were waited for; matrix products, arithmetic and copies ran while one was open for 0% of the time, Pallas kernels for 0%

commit v1 on v0

v1 whole, which is shorter than its diff:
```python
import functools

import jax
import jax.numpy as jnp
from jax import lax
from jax.experimental import pallas as pl
from jax.experimental.pallas import tpu as pltpu
from jax.sharding import PartitionSpec as P

F32, BF16 = jnp.float32, jnp.bfloat16
MESH = pl.DeviceIdType.MESH
NT = (((1,), (1,)), ((), ()))
TN = (((0,), (0,)), ((), ()))
LANES = 128
SLOT_ROWS = 32
UNIT_GROUP = 2
RING_EVERY = 3


def rdma(src, dst, send_sem, recv_sem, device):
    return pltpu.make_async_remote_copy(
        src_ref=src, dst_ref=dst, send_sem=send_sem, recv_sem=recv_sem,
        device_id=device, device_id_type=MESH,
    )


def iota(shape, dim):
    return lax.broadcasted_iota(jnp.int32, shape, dim)


def steps(start, stop, body):
    def run(i, carry):
        body(i)
        return carry

    lax.fori_loop(start, stop, run, 0)


def whitening(gram):
    half = gram.shape[0] // 2
    lane, row = iota((half, LANES), 1), iota((half, LANES), 0)
    low = lane < half
    eye = jnp.where((lane == row) | (lane == row + half), 1.0, 0.0).astype(F32)
    tables = [jnp.where(low, gram[:half], eye), jnp.where(low, eye, gram[half:])]
    blocks = [[t[8 * b : 8 * b + 8] for b in range(half // 8)] for t in tables]
    sub = iota((8, LANES), 0)
    for k in range(half):
        own, at = k // 8, k % 8
        for which in range(2):
            parts = blocks[which]
            pivot_lane = k + which * half
            pivot_row = parts[own][at : at + 1, :]
            scaled = pivot_row / pivot_row[:, pivot_lane : pivot_lane + 1]
            for b in range(own, half // 8):
                column = parts[b][:, pivot_lane : pivot_lane + 1]
                update = column * scaled
                if b == own:
                    update = jnp.where(sub > at, update, 0.0)
                parts[b] = parts[b] - update
    done = [jnp.concatenate(parts, axis=0) for parts in blocks]
    result = []
    for which in range(2):
        diag = jnp.sum(
            jnp.where(lane == row + which * half, done[which], 0.0), axis=1, keepdims=True
        )
        moved = pltpu.roll(done[which] * lax.rsqrt(diag), half, 1)
        result.append(jnp.where(low if which == 0 else jnp.logical_not(low), moved, 0.0))
    return jnp.concatenate(result, axis=0)


def kernel(
    dims,
    cot, ids, gts, qt, hid,
    p_out, q_out,
    cotb, gb, rmat, cmat, emat, etmat, disp, qb, sbuf, rb, zs, pz, hv, p640,
    ptp, prb, pfull, btr, zs2, mz, mg, ybuf, qp, qh, fs, fr, bs, br,
    hsem, s_cot, r_cot, s_g, r_g, s_q, r_q, s_qp, r_qp, s_rs, r_rs, s_z, r_z,
    s_p, r_p, s_pf, r_pf, s_m, r_m, s_mg, r_mg, s_h, r_h, s_f, r_f, s_b, r_b,
):
    G, J, cap = dims
    Z, U = J // 2, J // 4
    V = max(1, U // UNIT_GROUP)
    UG = U // V
    T, width = cot.shape
    Dd = width // G
    unit = 4 * cap
    half = 2 * cap
    GB = min(4, G)
    R8 = LANES // G
    FF = hid.shape[-1]
    g = lax.axis_index("dp")
    j = lax.axis_index("expert")
    z, c = lax.div(j, 2), lax.rem(j, 2)
    mate = j + 1 - 2 * c
    up = lax.rem(z + 1, Z) * 2 + c
    down = lax.rem(z + Z - 1, Z) * 2 + c

    def dp(k):
        return lax.rem(g + k, G)

    def chip(m):
        return lax.rem(z + ((m + 1) // 2 if m % 2 else Z - m // 2), Z)

    hcopy = pltpu.make_async_copy(hid.at[:, 0], hv, hsem)
    hcopy.start()

    barrier = pltpu.get_barrier_semaphore()

    def greet_dp(k):
        pl.semaphore_signal(barrier, inc=1, device_id={"dp": dp(k)}, device_id_type=MESH)

    def greet_expert(k):
        pl.semaphore_signal(
            barrier, inc=1, device_id={"expert": lax.rem(j + k, J)}, device_id_type=MESH
        )

    steps(1, G, greet_dp)
    steps(1, J, greet_expert)

    lane_t = iota((T, LANES), 1)
    gate = jnp.zeros((T, LANES), F32)
    named = jnp.zeros((T, LANES), F32)
    for k in range(ids.shape[1]):
        one = ids[:, k : k + 1]
        gate = gate + jnp.where(lane_t == one, gts[:, k : k + 1].astype(F32), 0.0)
        named = named + jnp.where(lane_t == one + 64, 1.0, 0.0)
    earlier = jnp.where(iota((T, T), 1) < iota((T, T), 0), 1.0, 0.0).astype(BF16)
    slots = jnp.dot(earlier, named.astype(BF16), preferred_element_type=F32)
    gb[g] = jnp.where(lane_t < 64, gate, slots).astype(BF16)

    r80, l80 = iota((unit, LANES), 0), iota((unit, LANES), 1)
    core80 = jnp.where((r80 >= cap) & (r80 < half), 1, 0) + jnp.where(r80 >= half + cap, 1, 0)
    h80 = jnp.where(r80 >= half, 1, 0)
    base80 = 2 * core80 + h80
    slot80 = r80 - cap * core80 - half * h80
    for i in range(4):
        cmat[unit * i : unit * (i + 1), :] = slot80.astype(F32)
    for m in range(Z):
        rmat[unit * m : unit * (m + 1), :] = jnp.where(
            l80 == base80 + 4 * chip(m), 1.0, 0.0
        ).astype(BF16)
    er, el = iota((LANES, LANES), 0), iota((LANES, LANES), 1)
    eblk = (
        jnp.where(er >= SLOT_ROWS, 1, 0)
        + jnp.where(er >= 2 * SLOT_ROWS, 1, 0)
        + jnp.where(er >= 3 * SLOT_ROWS, 1, 0)
    )
    inside = er - SLOT_ROWS * eblk
    emat[...] = jnp.where((inside < cap) & (el == inside + cap * eblk), 1.0, 0.0).astype(BF16)
    tblk = (
        jnp.where(r80 >= cap, 1, 0)
        + jnp.where(r80 >= 2 * cap, 1, 0)
        + jnp.where(r80 >= 3 * cap, 1, 0)
    )
    etmat[...] = jnp.where(l80 == r80 + (SLOT_ROWS - cap) * tblk, 1.0, 0.0).astype(BF16)

    pl.semaphore_wait(barrier, G + J - 2)

    def cot_copy(k):
        d = dp(k)
        return rdma(
            cot.at[:, pl.ds(pl.multiple_of(d * Dd, Dd), Dd)], cotb.at[g],
            s_cot.at[k], r_cot.at[g], {"dp": d},
        )

    def g_copy(k):
        return rdma(gb.at[g], gb.at[g], s_g.at[k], r_g.at[g], {"dp": dp(k)})

    def ring_copy(src, m, sem_at, device):
        return rdma(src, qb.at[m, c], s_q.at[sem_at], r_q.at[m], {"expert": device})

    def mate_copy(src, m):
        return rdma(src, qb.at[m, c], s_qp.at[m], r_qp.at[m], {"expert": mate})

    def ring_first():
        ring_copy(qt, 1, 1, down).start()
        if Z > 2:
            ring_copy(qt, 2, 2, up).start()
        mate_copy(qt, 0).start()

    ring_first()

    def send_cot(k):
        g_copy(k).start()
        cot_copy(k).start()

    steps(1, G, send_cot)
    qb[0, c] = qt[...]
    cotb[g] = cot[:, pl.ds(pl.multiple_of(g * Dd, Dd), Dd)]

    def ring_step(s):
        m = 2 * s - 1
        ring_copy(qb.at[m, c], m, m, down).wait_recv()

        @pl.when(s < Z // 2)
        def _():
            ring_copy(qb.at[m, c], m + 2, m + 2, down).start()

        mate_copy(qb.at[m, c], m).start()

        @pl.when(s < Z // 2)
        def _():
            n = 2 * s
            ring_copy(qb.at[n, c], n, n, up).wait_recv()

            @pl.when(s < Z // 2 - 1)
            def _():
                ring_copy(qb.at[n, c], n + 2, n + 2, up).start()

            mate_copy(qb.at[n, c], n).start()

    early = min((G - 1) // RING_EVERY, Z // 2)
    QC = min(4, Z)
    rows_q = unit * QC

    def dispatch_step(k):
        src = lax.rem(g + G - k, G)

        @pl.when(k > 0)
        def _():
            rdma(gb.at[src], gb.at[src], s_g.at[k], r_g.at[src], {"dp": src}).wait_recv()
            rdma(cotb.at[src], cotb.at[src], s_cot.at[k], r_cot.at[src], {"dp": src}).wait_recv()

        table = gb[src].astype(F32)
        both = jnp.concatenate([table, pltpu.roll(table, 64, 1)], axis=0).astype(BF16)
        tokens = cotb[src]

        def block(i):
            at = pl.multiple_of(i * rows_q, rows_q)
            spread = lax.dot_general(
                rmat[pl.ds(at, rows_q), :], both, NT, preferred_element_type=F32
            )
            hit = spread[:, T:] == cmat[:rows_q, :]
            chooser = jnp.where(hit, spread[:, :T], 0.0).astype(BF16)
            rows = jnp.dot(chooser, tokens, preferred_element_type=F32).astype(BF16)
            for n in range(QC):
                disp[i * QC + n, pl.ds(pl.multiple_of(src * unit, unit), unit), :] = rows[
                    unit * n : unit * (n + 1)
                ]

        steps(0, Z // QC, block)

        @pl.when((k > 0) & (lax.rem(k, RING_EVERY) == 0) & (k <= RING_EVERY * early))
        def _():
            ring_step(lax.div(k, RING_EVERY))

    steps(0, G, dispatch_step)

    first_core = (r80 < cap) | ((r80 >= half) & (r80 < half + cap))
    low40 = iota((half, LANES), 1) < 64

    def rs_copy(k, v):
        d = dp(k)
        return rdma(
            sbuf.at[d, pl.ds(v * UG, UG)], rb.at[g, pl.ds(v * UG, UG)],
            s_rs.at[k, v], r_rs.at[g, v], {"dp": d},
        )

    def project_unit(u):
        @pl.when(u + 1 > early)
        def _():
            ring_step(u + 1)

        for par in range(2):
            m = 2 * u + par
            rdma(qb.at[m, 1 - c], qb.at[m, 1 - c], s_qp.at[m], r_qp.at[m], {"expert": mate}).wait_recv()

        def batch(b):
            outs = []
            for par in range(2):
                m = 2 * u + par
                rows = disp[m, pl.ds(pl.multiple_of(b * GB * unit, GB * unit), GB * unit), :]
                x = lax.dot_general(
                    rows, qb[m].reshape(2 * LANES, Dd), NT, preferred_element_type=F32
                )
                picked = []
                for i in range(GB):
                    one = x[unit * i : unit * (i + 1)]
                    sel = jnp.where(first_core, one[:, :LANES], one[:, LANES:])
                    picked.append(jnp.where(low40, sel[:half], sel[half:]))
                outs.append(picked)
            for i in range(GB):
                sbuf[b * GB + i, u] = jnp.concatenate([outs[0][i], outs[1][i]], axis=0).astype(BF16)

        steps(0, G // GB, batch)

        @pl.when(lax.rem(u + 1, UG) == 0)
        def _():
            v = lax.div(u, UG)
            steps(1, G, lambda k: rs_copy(k, v).start())

    steps(0, U, project_unit)

    def z_copy(m, core):
        return rdma(
            zs.at[m, core], pz.at[j], s_z.at[m, core], r_z.at[j],
            {"expert": chip(m) * 2 + core},
        )

    pad = jnp.zeros((LANES - unit, LANES), BF16)
    for v in range(V):

        def add(k, acc):
            src = lax.rem(g + G - k, G)
            rdma(
                rb.at[src, pl.ds(v * UG, UG)], rb.at[src, pl.ds(v * UG, UG)],
                s_rs.at[k, v], r_rs.at[src, v], {"dp": src},
            ).wait_recv()
            return acc + rb[src, pl.ds(v * UG, UG)].astype(F32)

        total = lax.fori_loop(1, G, add, sbuf[g, pl.ds(v * UG, UG)].astype(F32))
        for i in range(UG):
            u = v * UG + i
            rows = jnp.concatenate([total[i].astype(BF16), pad], axis=0)
            spread = jnp.dot(emat[...], rows, preferred_element_type=F32).astype(BF16)
            for b in range(4):
                m, core = 2 * u + b // 2, b % 2
                zs[m, core] = spread[SLOT_ROWS * b : SLOT_ROWS * (b + 1)]
                if m == 0:

                    @pl.when(c == core)
                    def _():
                        pz[j] = spread[SLOT_ROWS * b : SLOT_ROWS * (b + 1)]

                    @pl.when(c != core)
                    def _():
                        z_copy(m, core).start()
                else:
                    z_copy(m, core).start()

    def z_wait(k):
        src = lax.rem(j + k, J)
        rdma(pz.at[src], pz.at[src], s_z.at[0, 0], r_z.at[src], {"expert": src}).wait_recv()

    steps(1, J, z_wait)

    for q in range(U):
        blocks = pz[4 * q : 4 * q + 4].reshape(LANES, LANES)
        p640[unit * q : unit * (q + 1), :] = jnp.dot(
            etmat[...], blocks, preferred_element_type=F32
        ).astype(BF16)
    hcopy.wait()
    turned = p640[...].astype(F32).T.astype(BF16)
    for h in range(2):
        ptp[64 * h : 64 * (h + 1), :] = jnp.dot(
            turned[64 * h : 64 * (h + 1)], hv[h], preferred_element_type=F32
        )

    def p_copy(k):
        d = dp(k)
        return rdma(
            ptp.at[pl.ds(pl.multiple_of(d * R8, R8), R8), :], prb.at[g],
            s_p.at[k], r_p.at[g], {"dp": d},
        )

    def share(at):
        return pfull.at[pl.ds(pl.multiple_of(at * R8, R8), R8), :]

    def pf_copy(k):
        return rdma(share(g), share(g), s_pf.at[k], r_pf.at[g], {"dp": dp(k)})

    steps(1, G, lambda k: p_copy(k).start())

    def add_p(k, acc):
        src = lax.rem(g + G - k, G)
        rdma(prb.at[src], prb.at[src], s_p.at[k], r_p.at[src], {"dp": src}).wait_recv()
        return acc + prb[src]

    own_rows = pl.ds(pl.multiple_of(g * R8, R8), R8)
    pfull[own_rows, :] = lax.fori_loop(1, G, add_p, ptp[own_rows, :])
    steps(1, G, lambda k: pf_copy(k).start())

    def pf_wait(k):
        src = lax.rem(g + G - k, G)
        rdma(share(src), share(src), s_pf.at[k], r_pf.at[src], {"dp": src}).wait_recv()

    steps(1, G, pf_wait)

    full = pfull[...]
    gram = lax.dot_general(
        full, full, NT, precision=lax.Precision.HIGHEST, preferred_element_type=F32
    )
    inverse = whitening(gram)
    btr[...] = jnp.dot(
        inverse, full, precision=lax.Precision.HIGHEST, preferred_element_type=F32
    ).astype(BF16)

    QB = min(4, U)
    rows_m = QB * unit
    low_m = iota((rows_m, LANES), 1) < 64

    def map_block(i):
        at = pl.multiple_of(i * rows_m, rows_m)
        found = [
            lax.dot_general(
                hv[h, pl.ds(at, rows_m), :], btr[...], NT, preferred_element_type=F32
            )
            for h in range(2)
        ]
        rows = jnp.where(low_m, found[0], found[1]).astype(BF16)
        for q in range(QB):
            padded = jnp.concatenate([rows[unit * q : unit * (q + 1)], pad], axis=0)
            spread = jnp.dot(emat[...], padded, preferred_element_type=F32).astype(BF16)
            for b in range(4):
                zs2[(i * QB + q) * 4 + b] = spread[SLOT_ROWS * b : SLOT_ROWS * (b + 1)]

    steps(0, U // QB, map_block)

    def back_index(m):
        if m == Z - 1:
            return m
        return m + 1 if m % 2 else max(m - 1, 0)

    def m_copy(m, core):
        target = chip(m) * 2 + core
        return rdma(
            zs2.at[target], mz.at[back_index(m), c], s_m.at[m, core],
            r_m.at[back_index(m), c], {"expert": target},
        )

    for m in reversed(range(Z)):
        for core in range(2):
            if m == 0:

                @pl.when(c == core)
                def _():
                    mz[0, c] = zs2[j]

                @pl.when(c != core)
                def _():
                    m_copy(0, core).start()
            else:
                m_copy(m, core).start()

    def m_wait(m, core):
        rdma(
            mz.at[m, core], mz.at[m, core], s_m.at[m, core], r_m.at[m, core],
            {"expert": mate},
        ).wait_recv()

    def mg_copy(k, v):
        part = mg.at[g, pl.ds(v * UG, UG)]
        return rdma(part, part, s_mg.at[k, v], r_mg.at[g, v], {"dp": dp(k)})

    for v in reversed(range(V)):
        for u in reversed(range(v * UG, (v + 1) * UG)):
            for b in range(4):
                m, core = 2 * u + b // 2, b % 2
                if m == 0:

                    @pl.when(c != core)
                    def _():
                        m_wait(0, core)
                else:
                    m_wait(m, core)
            blocks = mz[2 * u : 2 * u + 2].reshape(LANES, LANES)
            mg[g, u] = jnp.dot(etmat[...], blocks, preferred_element_type=F32).astype(BF16)
        steps(1, G, lambda k: mg_copy(k, v).start())

    low_core = first_core[:half]
    keep = [
        [low40 & low_core, low40 & jnp.logical_not(low_core)],
        [jnp.logical_not(low40) & low_core, jnp.logical_not(low40) & jnp.logical_not(low_core)],
    ]

    def half_copy(m):
        return rdma(qp.at[m, 1 - c], qh.at[m], s_h.at[m], r_h.at[m], {"expert": mate})

    def up_copy(s):
        return rdma(fs.at[s - 1], fr.at[s - 1], s_f.at[s - 1], r_f.at[s - 1], {"expert": up})

    def down_copy(s):
        return rdma(bs.at[s - 1], br.at[s - 1], s_b.at[s - 1], r_b.at[s - 1], {"expert": down})

    def sum_step(s):
        m = 2 * (U + 1 - s) - 1
        half_copy(m).wait_recv()
        value = qp[m, c] + qh[m]

        @pl.when(s > 1)
        def _():
            up_copy(s - 1).wait_recv()
            fs[s - 1] = value + fr[s - 2]

        @pl.when(s <= 1)
        def _():
            fs[s - 1] = value

        up_copy(s).start()

        @pl.when(s < U)
        def _():
            n = 2 * (U - s)
            half_copy(n).wait_recv()
            other = qp[n, c] + qh[n]

            @pl.when(s > 1)
            def _():
                down_copy(s - 1).wait_recv()
                bs[s - 1] = other + br[s - 2]

            @pl.when(s <= 1)
            def _():
                bs[s - 1] = other

            down_copy(s).start()

    def factor_unit(i):
        u = U - 1 - i

        @pl.when(lax.rem(i, UG) == 0)
        def _():
            v = lax.div(u, UG)

            def wait(k):
                src = lax.rem(g + G - k, G)
                part = mg.at[src, pl.ds(v * UG, UG)]
                rdma(part, part, s_mg.at[k, v], r_mg.at[src, v], {"dp": src}).wait_recv()

            steps(1, G, wait)

        def spread(b):
            rows = mg[b, u].astype(F32)
            for par in range(2):
                one = rows[half * par : half * (par + 1)]
                wide = [
                    jnp.concatenate([jnp.where(keep[h][core], one, 0.0) for h in range(2)], axis=0)
                    for core in range(2)
                ]
                at = pl.ds(pl.multiple_of(b * unit, unit), unit)
                ybuf[par, at, 0:LANES] = wide[0].astype(BF16)
                ybuf[par, at, LANES : 2 * LANES] = wide[1].astype(BF16)

        steps(0, G, spread)
        for par in range(2):
            m = 2 * u + par
            found = lax.dot_general(ybuf[par], disp[m], TN, preferred_element_type=F32)
            qp[m, 0] = found[:LANES]
            qp[m, 1] = found[LANES:]
            half_copy(m).start()

        @pl.when(i > 0)
        def _():
            sum_step(i)

    steps(0, U, factor_unit)
    sum_step(U)
    half_copy(0).wait_recv()
    total = qp[0, c] + qh[0]
    if U > 1:
        down_copy(U - 1).wait_recv()
        total = total + br[U - 2]
    up_copy(U).wait_recv()
    q_out[...] = total + fr[U - 1]

    share_cols = FF // G
    start = g * share_cols
    tile = jnp.minimum(lax.div(start, LANES), FF // LANES - 2)
    window = pfull[:, pl.ds(pl.multiple_of(tile * LANES, LANES), 2 * LANES)]
    shift = lax.rem(3 * LANES + tile * LANES - start - LANES + 2 * LANES, 2 * LANES)
    p_out[...] = pltpu.roll(window, shift, 1)[:, :share_cols]

    def drain_dp(k):
        g_copy(k).wait_send()
        cot_copy(k).wait_send()
        p_copy(k).wait_send()
        pf_copy(k).wait_send()
        for v in range(V):
            rs_copy(k, v).wait_send()
            mg_copy(k, v).wait_send()

    steps(1, G, drain_dp)

    def drain_ring(m):
        ring_copy(qt, m, m, up).wait_send()

    steps(1, Z, drain_ring)

    def drain_mate(m):
        mate_copy(qt, m).wait_send()
        half_copy(m).wait_send()

    steps(0, Z, drain_mate)
    for m in range(Z):
        for core in range(2):
            if m == 0:

                @pl.when(c != core)
                def _():
                    z_copy(0, core).wait_send()
                    m_copy(0, core).wait_send()
            else:
                z_copy(m, core).wait_send()
                m_copy(m, core).wait_send()
    steps(1, U + 1, lambda s: up_copy(s).wait_send())
    steps(1, U, lambda s: down_copy(s).wait_send())


def local(cotangent, expert_ids, gates, hidden, q_prev):
    G, J = lax.axis_size("dp"), lax.axis_size("expert")
    T, width = cotangent.shape
    rows, FF = hidden.shape[2], hidden.shape[3]
    cap = rows // J
    rank = q_prev.shape[2]
    Dd = width // G
    Z, U = J // 2, J // 4
    V = max(1, U // UNIT_GROUP)
    unit = 4 * cap
    qt = jnp.swapaxes(q_prev, 1, 2).reshape(2 * rank, Dd)
    vm, sem = pltpu.VMEM, pltpu.SemaphoreType.DMA
    scratch = [
        vm((G, T, Dd), BF16),
        vm((G, T, LANES), BF16),
        vm((Z * unit, LANES), BF16),
        vm((4 * unit, LANES), F32),
        vm((LANES, LANES), BF16),
        vm((unit, LANES), BF16),
        vm((Z, G * unit, Dd), BF16),
        vm((Z, 2, LANES, Dd), BF16),
        vm((G, U, unit, LANES), BF16),
        vm((G, U, unit, LANES), BF16),
        vm((Z, 2, SLOT_ROWS, LANES), BF16),
        vm((J, SLOT_ROWS, LANES), BF16),
        vm((2, rows, FF), BF16),
        vm((rows, LANES), BF16),
        vm((LANES, FF), F32),
        vm((G, LANES // G, FF), F32),
        vm((LANES, FF), F32),
        vm((LANES, FF), BF16),
        vm((J, SLOT_ROWS, LANES), BF16),
        vm((Z, 2, SLOT_ROWS, LANES), BF16),
        vm((G, U, unit, LANES), BF16),
        vm((2, G * unit, 2 * LANES), BF16),
        vm((Z, 2, LANES, Dd), F32),
        vm((Z, LANES, Dd), F32),
        vm((U, LANES, Dd), F32),
        vm((U, LANES, Dd), F32),
        vm((max(1, U - 1), LANES, Dd), F32),
        vm((max(1, U - 1), LANES, Dd), F32),
        pltpu.SemaphoreType.DMA,
        sem((G,)), sem((G,)), sem((G,)), sem((G,)),
        sem((Z,)), sem((Z,)), sem((Z,)), sem((Z,)),
        sem((G, V)), sem((G, V)),
        sem((Z, 2)), sem((J,)),
        sem((G,)), sem((G,)), sem((G,)), sem((G,)),
        sem((Z, 2)), sem((Z, 2)),
        sem((G, V)), sem((G, V)),
        sem((Z,)), sem((Z,)),
        sem((U,)), sem((U,)), sem((max(1, U - 1),)), sem((max(1, U - 1),)),
    ]
    full = pl.BlockSpec(memory_space=pltpu.VMEM)
    p_t, q_t = pl.pallas_call(
        functools.partial(kernel, (G, J, cap)),
        out_shape=(
            jax.ShapeDtypeStruct((LANES, FF // G), F32),
            jax.ShapeDtypeStruct((LANES, Dd), F32),
        ),
        in_specs=[full, full, full, full, pl.BlockSpec(memory_space=pl.ANY)],
        out_specs=(full, full),
        scratch_shapes=scratch,
        compiler_params=pltpu.CompilerParams(
            collective_id=0, has_side_effects=True, vmem_limit_bytes=60 * 2**20
        ),
    )(cotangent, expert_ids, gates, qt, hidden)
    p_share = jnp.swapaxes(p_t.reshape(2, rank, FF // G), 1, 2)
    q_share = jnp.swapaxes(q_t.reshape(2, rank, Dd), 1, 2)
    return (p_share, q_share)


def solution(mesh):
    placed = (
        P(("dp", "expert"), None),
        P(("dp", "expert"), None),
        P(("dp", "expert"), None),
        P("expert", "dp", None, None),
        P("expert", "dp", None),
    )
    return jax.shard_map(
        local,
        mesh=mesh,
        in_specs=placed,
        out_specs=(P("expert", "dp", None), P("expert", "dp", None)),
        check_vma=False,
    )
```

time: 829 us -> 212 us (0.26)
  the two profiles are of different devices: /device:TPU:6 before, /device:TPU:86 now
where the time goes in v1:
time: 212 us
  Pallas kernels  205 us (97%)
  local copies, waits for them, and re-layouts  5.85 us (3%)
    pallas_call x1, Pallas kernels, local(): pl.pallas_call(functools.partial(kernel, (G, J, cap)), out_shape=(jax.Sha...  205 us
    unnamed x4, local copies, waits for them, and re-layouts  5.85 us

profile of v1, /device:TPU:86, one launch (start us, length us, event | category | flops | bytes accessed | tf_op | source)
XLA Modules:
  0.0 211.6 jit_solution(4050647125634631718)
XLA Ops:
  0.6 1.4 copy.8.gts
  2.0 1.4 copy.7.ids
  3.4 205.1 %shard_map.68 = (f32[128,96]{1,0:T(8,128)}, f32[128,256]{1,0:T(8,128)}) custom-call(bf16[128,4096]{1,0:T(8,128)(2,1)} %cot.1, s32[128,8]{1,0:T(8,128)} %copy.7.ids, bf16[128,8]{1,0:T(8,128)(2,1)} %copy.8.gts, bf16[128,256]{1,0:T(8,128)(2,1)} %bitcast.10, bf16[2,1,640,1536]{3,2,1,0:T(8,128)(2,1)} %hid.1), custom_call_target="tpu_custom_call" | custom-call | tf_op jit(solution)/shard_map/pallas_call | solution.py:652
  208.5 1.5 copy.11
  210.0 1.6 copy.12

commit v2 on v1

--- a/solution.py
+++ b/solution.py
@@ -14,7 +14,10 @@
 LANES = 128
 SLOT_ROWS = 32
 UNIT_GROUP = 2
-RING_EVERY = 3
+SIDE = 4
+RING_EVERY = 5
+RING_FIRST = 4
+TABLE_ROWS = 16
 
 
 def rdma(src, dst, send_sem, recv_sem, device):
@@ -72,8 +75,8 @@
     dims,
     cot, ids, gts, qt, hid,
     p_out, q_out,
-    cotb, gb, rmat, cmat, emat, etmat, disp, qb, sbuf, rb, zs, pz, hv, p640,
-    ptp, prb, pfull, btr, zs2, mz, mg, ybuf, qp, qh, fs, fr, bs, br,
+    cotb, gb, erel, tabg, tabs, emat, etmat, disp, qb, sbuf, rb, zs, pz, hv, p640,
+    ptp, prb, pfull, btr, zs2, mz, mg, ybuf, qp, qh, f16s, f16r, f32s, f32r, b16s, b16r, b32s, b32r, work,
     hsem, s_cot, r_cot, s_g, r_g, s_q, r_q, s_qp, r_qp, s_rs, r_rs, s_z, r_z,
     s_p, r_p, s_pf, r_pf, s_m, r_m, s_mg, r_mg, s_h, r_h, s_f, r_f, s_b, r_b,
 ):
@@ -117,28 +120,18 @@
     steps(1, G, greet_dp)
     steps(1, J, greet_expert)
 
-    lane_t = iota((T, LANES), 1)
-    gate = jnp.zeros((T, LANES), F32)
-    named = jnp.zeros((T, LANES), F32)
-    for k in range(ids.shape[1]):
-        one = ids[:, k : k + 1]
-        gate = gate + jnp.where(lane_t == one, gts[:, k : k + 1].astype(F32), 0.0)
-        named = named + jnp.where(lane_t == one + 64, 1.0, 0.0)
-    earlier = jnp.where(iota((T, T), 1) < iota((T, T), 0), 1.0, 0.0).astype(BF16)
-    slots = jnp.dot(earlier, named.astype(BF16), preferred_element_type=F32)
-    gb[g] = jnp.where(lane_t < 64, gate, slots).astype(BF16)
-
+    gb[g] = jnp.concatenate([ids[...].astype(F32), gts[...].astype(F32)], axis=0).astype(BF16)
+
+    sub = iota((8, LANES), 0)
+    for i in range(Z // 2):
+        near = jnp.where(sub < 4, 4 * chip(2 * i), 4 * chip(2 * i + 1) - 4)
+        erel[8 * i : 8 * i + 8, :] = (near + sub).astype(F32)
+    before = jnp.where(iota((T, T), 0) < iota((T, T), 1), 1.0, 0.0).astype(BF16)
+    slot_rows = [
+        value.astype(F32)
+        for value in (sub, sub + 8, jnp.where(sub < 4, sub + 16, sub - 4), sub + 4, sub + 12)
+    ]
     r80, l80 = iota((unit, LANES), 0), iota((unit, LANES), 1)
-    core80 = jnp.where((r80 >= cap) & (r80 < half), 1, 0) + jnp.where(r80 >= half + cap, 1, 0)
-    h80 = jnp.where(r80 >= half, 1, 0)
-    base80 = 2 * core80 + h80
-    slot80 = r80 - cap * core80 - half * h80
-    for i in range(4):
-        cmat[unit * i : unit * (i + 1), :] = slot80.astype(F32)
-    for m in range(Z):
-        rmat[unit * m : unit * (m + 1), :] = jnp.where(
-            l80 == base80 + 4 * chip(m), 1.0, 0.0
-        ).astype(BF16)
     er, el = iota((LANES, LANES), 0), iota((LANES, LANES), 1)
     eblk = (
         jnp.where(er >= SLOT_ROWS, 1, 0)
@@ -209,9 +202,10 @@
 
             mate_copy(qb.at[n, c], n).start()
 
-    early = min((G - 1) // RING_EVERY, Z // 2)
+    first_steps = min(RING_FIRST, Z // 2)
+    early = min(first_steps + G // RING_EVERY, Z // 2)
     QC = min(4, Z)
-    rows_q = unit * QC
+    steps(1, first_steps + 1, ring_step)
 
     def dispatch_step(k):
         src = lax.rem(g + G - k, G)
@@ -222,27 +216,38 @@
             rdma(cotb.at[src], cotb.at[src], s_cot.at[k], r_cot.at[src], {"dp": src}).wait_recv()
 
         table = gb[src].astype(F32)
-        both = jnp.concatenate([table, pltpu.roll(table, 64, 1)], axis=0).astype(BF16)
+        found = jnp.zeros(tabg.shape, F32)
+        wanted = erel[...]
+        for n in range(TABLE_ROWS // 2):
+            hit = table[n : n + 1, :] == wanted
+            found = jnp.where(hit, table[TABLE_ROWS // 2 + n : TABLE_ROWS // 2 + n + 1, :], found)
+        tabg[...] = found
+        named = jnp.where(found > 0.0, 1.0, 0.0).astype(BF16)
+        tabs[...] = jnp.dot(named, before, preferred_element_type=F32)
         tokens = cotb[src]
-
-        def block(i):
-            at = pl.multiple_of(i * rows_q, rows_q)
-            spread = lax.dot_general(
-                rmat[pl.ds(at, rows_q), :], both, NT, preferred_element_type=F32
-            )
-            hit = spread[:, T:] == cmat[:rows_q, :]
-            chooser = jnp.where(hit, spread[:, :T], 0.0).astype(BF16)
+        at = pl.ds(pl.multiple_of(src * unit, unit), unit)
+
+        def wide(ref, row):
+            return jnp.broadcast_to(ref[row : row + 1, :], (8, LANES))
+
+        for m0 in range(0, Z, QC):
+            pieces = []
+            for m in range(m0, m0 + QC):
+                for h in range(2):
+                    gate = [wide(tabg, 4 * m + 2 * core + h) for core in range(2)]
+                    slot = [wide(tabs, 4 * m + 2 * core + h) for core in range(2)]
+                    gates = [gate[0], gate[0], jnp.where(sub < 4, *gate), gate[1], gate[1]]
+                    slots = [slot[0], slot[0], jnp.where(sub < 4, *slot), slot[1], slot[1]]
+                    for n in range(5):
+                        pieces.append(jnp.where(slots[n] == slot_rows[n], gates[n], 0.0))
+            chooser = jnp.concatenate(pieces, axis=0).astype(BF16)
             rows = jnp.dot(chooser, tokens, preferred_element_type=F32).astype(BF16)
             for n in range(QC):
-                disp[i * QC + n, pl.ds(pl.multiple_of(src * unit, unit), unit), :] = rows[
-                    unit * n : unit * (n + 1)
-                ]
-
-        steps(0, Z // QC, block)
-
-        @pl.when((k > 0) & (lax.rem(k, RING_EVERY) == 0) & (k <= RING_EVERY * early))
-        def _():
-            ring_step(lax.div(k, RING_EVERY))
+                disp[m0 + n, at, :] = rows[unit * n : unit * (n + 1)]
+
+        @pl.when((lax.rem(k, RING_EVERY) == RING_EVERY - 1) & (k < RING_EVERY * (early - first_steps)))
+        def _():
+            ring_step(first_steps + lax.div(k + 1, RING_EVERY))
 
     steps(0, G, dispatch_step)
 
@@ -438,9 +443,61 @@
             {"expert": mate},
         ).wait_recv()
 
-    def mg_copy(k, v):
-        part = mg.at[g, pl.ds(v * UG, UG)]
-        return rdma(part, part, s_mg.at[k, v], r_mg.at[g, v], {"dp": dp(k)})
+    gx, gy = lax.rem(g, SIDE), lax.div(g, SIDE)
+
+    def place(v, da, db):
+        flip = lax.rem(v, 2)
+        dx = (1 - flip) * da + flip * db
+        dy = flip * da + (1 - flip) * db
+        return lax.rem(gy + dy, SIDE) * SIDE + lax.rem(gx + dx, SIDE)
+
+    def piece(v, par, da, db, slot, ta, tb):
+        part = mg.at[place(v, da, db), 2 * v + par]
+        return rdma(
+            part, part, s_mg.at[2 * v + par, slot], r_mg.at[place(v, da, db), 2 * v + par],
+            {"dp": place(v, ta, tb)},
+        )
+
+    def piece_wait(v, par, da, db):
+        piece(v, par, da, db, 0, 1, 0).wait_recv()
+
+    def gather_row(v):
+        for par in range(2):
+            piece(v, par, 0, 0, 0, 1, 0).start()
+            piece(v, par, 0, 0, 1, SIDE - 1, 0).start()
+
+    def gather_cross(v):
+        for par in range(2):
+            piece(v, par, 0, 0, 3, 0, 1).start()
+            piece(v, par, 0, 0, 4, 0, SIDE - 1).start()
+        for par in range(2):
+            for da in (1, SIDE - 1) if par else (SIDE - 1, 1):
+                piece_wait(v, par, da, 0)
+                if da == (1 if par else SIDE - 1):
+                    piece(v, par, da, 0, 2, SIDE - da, 0).start()
+                piece(v, par, da, 0, 3 + 2 * da, 0, 1).start()
+                piece(v, par, da, 0, 4 + 2 * da, 0, SIDE - 1).start()
+        for par in range(2):
+            piece_wait(v, par, 2, 0)
+            piece(v, par, 2, 0, 3 + 2 * 2, 0, 1).start()
+            piece(v, par, 2, 0, 4 + 2 * 2, 0, SIDE - 1).start()
+
+    def gather_far(v):
+        def one(da):
+            for par in range(2):
+                for db in (1, SIDE - 1) if par else (SIDE - 1, 1):
+                    piece_wait(v, par, da, db)
+                    if db == (1 if par else SIDE - 1):
+                        piece(v, par, da, db, 11 + da, 0, SIDE - db).start()
+
+        steps(0, SIDE, one)
+
+    def gather_end(v):
+        def one(da):
+            for par in range(2):
+                piece_wait(v, par, da, 2)
+
+        steps(0, SIDE, one)
 
     for v in reversed(range(V)):
         for u in reversed(range(v * UG, (v + 1) * UG)):
@@ -455,7 +512,9 @@
                     m_wait(m, core)
             blocks = mz[2 * u : 2 * u + 2].reshape(LANES, LANES)
             mg[g, u] = jnp.dot(etmat[...], blocks, preferred_element_type=F32).astype(BF16)
-        steps(1, G, lambda k: mg_copy(k, v).start())
+        gather_row(jnp.int32(v))
+    steps(0, V, lambda i: gather_cross(V - 1 - i))
+    gather_far(jnp.int32(V - 1))
 
     low_core = first_core[:half]
     keep = [
@@ -466,44 +525,58 @@
     def half_copy(m):
         return rdma(qp.at[m, 1 - c], qh.at[m], s_h.at[m], r_h.at[m], {"expert": mate})
 
-    def up_copy(s):
-        return rdma(fs.at[s - 1], fr.at[s - 1], s_f.at[s - 1], r_f.at[s - 1], {"expert": up})
-
-    def down_copy(s):
-        return rdma(bs.at[s - 1], br.at[s - 1], s_b.at[s - 1], r_b.at[s - 1], {"expert": down})
-
-    def sum_step(s):
-        m = 2 * (U + 1 - s) - 1
-        half_copy(m).wait_recv()
-        value = qp[m, c] + qh[m]
-
-        @pl.when(s > 1)
-        def _():
-            up_copy(s - 1).wait_recv()
-            fs[s - 1] = value + fr[s - 2]
-
-        @pl.when(s <= 1)
-        def _():
-            fs[s - 1] = value
-
-        up_copy(s).start()
-
-        @pl.when(s < U)
-        def _():
-            n = 2 * (U - s)
-            half_copy(n).wait_recv()
-            other = qp[n, c] + qh[n]
+    class Chain:
+        def __init__(self, near, device, sends, gets, wide_sends, wide_gets, send_sem, get_sem):
+            self.near, self.device = near, device
+            self.narrow, self.wide = (sends, gets), (wide_sends, wide_gets)
+            self.sems = (send_sem, get_sem)
+
+        def copy(self, s, narrow):
+            sends, gets = self.narrow if narrow else self.wide
+            at = s - 1 if narrow else s - 1 - self.near
+            return rdma(
+                sends.at[at], gets.at[at], self.sems[0].at[s - 1], self.sems[1].at[s - 1],
+                {"expert": self.device},
+            )
+
+        def arrived(self, s):
+            @pl.when(s <= self.near)
+            def _():
+                self.copy(s, True).wait_recv()
+                work[...] = work[...] + self.narrow[1][s - 1].astype(F32)
+
+            @pl.when(s > self.near)
+            def _():
+                self.copy(s, False).wait_recv()
+                work[...] = work[...] + self.wide[1][s - 1 - self.near]
+
+        def send(self, m, s):
+            half_copy(m).wait_recv()
+            work[...] = qp[m, c] + qh[m]
 
             @pl.when(s > 1)
             def _():
-                down_copy(s - 1).wait_recv()
-                bs[s - 1] = other + br[s - 2]
-
-            @pl.when(s <= 1)
+                self.arrived(s - 1)
+
+            @pl.when(s <= self.near)
             def _():
-                bs[s - 1] = other
-
-            down_copy(s).start()
+                self.narrow[0][s - 1] = work[...].astype(BF16)
+                self.copy(s, True).start()
+
+            @pl.when(s > self.near)
+            def _():
+                self.wide[0][s - 1 - self.near] = work[...]
+                self.copy(s, False).start()
+
+    rise = Chain(max(1, U - 2), up, f16s, f16r, f32s, f32r, s_f, r_f)
+    fall = Chain(max(1, U - 3), down, b16s, b16r, b32s, b32r, s_b, r_b)
+
+    def sum_step(s):
+        rise.send(2 * (U + 1 - s) - 1, s)
+
+        @pl.when(s < U)
+        def _():
+            fall.send(2 * (U - s), s)
 
     def factor_unit(i):
         u = U - 1 - i
@@ -512,12 +585,11 @@
         def _():
             v = lax.div(u, UG)
 
-            def wait(k):
-                src = lax.rem(g + G - k, G)
-                part = mg.at[src, pl.ds(v * UG, UG)]
-                rdma(part, part, s_mg.at[k, v], r_mg.at[src, v], {"dp": src}).wait_recv()
-
-            steps(1, G, wait)
+            @pl.when(v > 0)
+            def _():
+                gather_far(v - 1)
+
+            gather_end(v)
 
         def spread(b):
             rows = mg[b, u].astype(F32)
@@ -544,14 +616,13 @@
             sum_step(i)
 
     steps(0, U, factor_unit)
-    sum_step(U)
+    sum_step(jnp.int32(U))
     half_copy(0).wait_recv()
-    total = qp[0, c] + qh[0]
+    work[...] = qp[0, c] + qh[0]
     if U > 1:
-        down_copy(U - 1).wait_recv()
-        total = total + br[U - 2]
-    up_copy(U).wait_recv()
-    q_out[...] = total + fr[U - 1]
+        fall.arrived(jnp.int32(U - 1))
+    rise.arrived(jnp.int32(U))
+    q_out[...] = work[...]
 
     share_cols = FF // G
     start = g * share_cols
@@ -567,7 +638,6 @@
         pf_copy(k).wait_send()
         for v in range(V):
             rs_copy(k, v).wait_send()
-            mg_copy(k, v).wait_send()
 
     steps(1, G, drain_dp)
 
@@ -592,8 +662,16 @@
             else:
                 z_copy(m, core).wait_send()
                 m_copy(m, core).wait_send()
-    steps(1, U + 1, lambda s: up_copy(s).wait_send())
-    steps(1, U, lambda s: down_copy(s).wait_send())
+    for s in range(1, U + 1):
+        rise.copy(s, s <= rise.near).wait_send()
+    for s in range(1, U):
+        fall.copy(s, s <= fall.near).wait_send()
+
+    def drain_gather(u):
+        for slot in range(15):
+            rdma(mg.at[g, u], mg.at[g, u], s_mg.at[u, slot], r_mg.at[g, u], {"dp": dp(1)}).wait_send()
+
+    steps(0, U, drain_gather)
 
 
 def local(cotangent, expert_ids, gates, hidden, q_prev):
@@ -606,13 +684,25 @@
     Z, U = J // 2, J // 4
     V = max(1, U // UNIT_GROUP)
     unit = 4 * cap
+    spare = ((0, TABLE_ROWS // 2 - expert_ids.shape[1]), (0, 0))
+    ids = jnp.pad(expert_ids.T, spare, constant_values=-1)
+    gts = jnp.pad(gates.T, spare)
     qt = jnp.swapaxes(q_prev, 1, 2).reshape(2 * rank, Dd)
+    near = (max(1, U - 2), max(1, U - 3))
+    sums = [
+        (n, kind)
+        for n, kind in (
+            (near[0], BF16), (near[0], BF16), (U - near[0], F32), (U - near[0], F32),
+            (near[1], BF16), (near[1], BF16), (U - 1 - near[1], F32), (U - 1 - near[1], F32),
+        )
+    ]
     vm, sem = pltpu.VMEM, pltpu.SemaphoreType.DMA
     scratch = [
         vm((G, T, Dd), BF16),
-        vm((G, T, LANES), BF16),
-        vm((Z * unit, LANES), BF16),
-        vm((4 * unit, LANES), F32),
+        vm((G, TABLE_ROWS, LANES), BF16),
+        vm((4 * Z, LANES), F32),
+        vm((4 * Z, LANES), F32),
+        vm((4 * Z, LANES), F32),
         vm((LANES, LANES), BF16),
         vm((unit, LANES), BF16),
         vm((Z, G * unit, Dd), BF16),
@@ -633,10 +723,8 @@
         vm((2, G * unit, 2 * LANES), BF16),
         vm((Z, 2, LANES, Dd), F32),
         vm((Z, LANES, Dd), F32),
-        vm((U, LANES, Dd), F32),
-        vm((U, LANES, Dd), F32),
-        vm((max(1, U - 1), LANES, Dd), F32),
-        vm((max(1, U - 1), LANES, Dd), F32),
+        *[vm((max(1, n), LANES, Dd), kind) for n, kind in sums],
+        vm((LANES, Dd), F32),
         pltpu.SemaphoreType.DMA,
         sem((G,)), sem((G,)), sem((G,)), sem((G,)),
         sem((Z,)), sem((Z,)), sem((Z,)), sem((Z,)),
@@ -644,7 +732,7 @@
         sem((Z, 2)), sem((J,)),
         sem((G,)), sem((G,)), sem((G,)), sem((G,)),
         sem((Z, 2)), sem((Z, 2)),
-        sem((G, V)), sem((G, V)),
+        sem((U, 15)), sem((G, U)),
         sem((Z,)), sem((Z,)),
         sem((U,)), sem((U,)), sem((max(1, U - 1),)), sem((max(1, U - 1),)),
     ]
@@ -661,7 +749,7 @@
         compiler_params=pltpu.CompilerParams(
             collective_id=0, has_side_effects=True, vmem_limit_bytes=60 * 2**20
         ),
-    )(cotangent, expert_ids, gates, qt, hidden)
+    )(cotangent, ids, gts, qt, hidden)
     p_share = jnp.swapaxes(p_t.reshape(2, rank, FF // G), 1, 2)
     q_share = jnp.swapaxes(q_t.reshape(2, rank, Dd), 1, 2)
     return (p_share, q_share)

time: 212 us -> 195 us (0.920)
  the two profiles are of different devices: /device:TPU:86 before, /device:TPU:6 now
where the time goes in v2:
time: 195 us; the launch traced here: 194 us
  Pallas kernels  191 us (98%)
  local copies, waits for them, and re-layouts  3.04 us (2%)
    pallas_call x1, Pallas kernels, local(): pl.pallas_call(functools.partial(kernel, (G, J, cap)), out_shape=(jax.Sha...  191 us

profile of v2, /device:TPU:6, one launch (start us, length us, event | category | flops | bytes accessed | tf_op | source)
XLA Modules:
  0.0 194.2 jit_solution(9714118277457472237)
XLA Ops:
  0.6 190.5 %shard_map.68 = (f32[128,96]{1,0:T(8,128)}, f32[128,256]{1,0:T(8,128)}) custom-call(bf16[128,4096]{1,0:T(8,128)(2,1)} %cot.1, s32[8,128]{1,0:T(8,128)} %bitcast.14, bf16[8,128]{1,0:T(8,128)(2,1)} %bitcast.15, bf16[128,256]{1,0:T(8,128)(2,1)} %bitcast.12, bf16[2,1,640,1536]{3,2,1,0:T(8,128)(2,1)} %hid.1), custom_call_target="tpu_custom_call" | custom-call | tf_op jit(solution)/shard_map/pallas_call | solution.py:740
  191.2 1.5 copy.9
  192.6 1.6 copy.10
